TPU v7x, 32 devices: a whole 2x2x4 slice. The times are simulated.
32 devices in a mesh: groups: 2 (over x), grid: 8 (over z, y), dp: 2 (over core).
Axes of the slice: x: 2, y: 2, z: 4, core: 2. Of those that a mesh axis runs over, the one named last changes fastest.
Arguments:
- rot_grads: bfloat16 [4096, 4096], P('grid', ('groups', 'dp')), parts along dimension 1, may hold values from -1 to 1
- rot_inputs: bfloat16 [28672, 4096], P('grid', ('groups', 'dp')), parts along dimension 1, may hold values from -6 to 6
- lengths: int32 [16], P(('groups', 'dp')), parts along dimension 0, may hold values from 1 to 256, as said below
- token_mask: int32 [4096], P(('groups', 'dp')), parts along dimension 0, may hold values 0 or 1
Outputs:
- correction: float32 [57344, 4096], P(('groups', 'grid'), 'dp'), parts along dimension 0
There are 2 independent parts, one for each index of `groups`. A program takes and returns all parts, laid end to end along the dimension named above; each array names one. Nothing has to cross between parts.
Inputs may be any that keep to these rules, and one draw needn't show every extreme that they name: `lengths`: each span holds at least one sequence token, and at least one span is full (256 tokens).
All inputs are finite; a program needn't handle non-finite values. No bound on the sum of `token_mask` on one device may be relied on, other than what follows from the above.
Results may differ from a plain program's by a relative error of at most 0.0003.
Values may be sent and summed in bfloat16 or wider, within the bound.
A program may use at most 448 MiB of HBM per device.

v0:
```python
import jax
import jax.numpy as jnp
from jax import lax
from jax.sharding import PartitionSpec as P

O = 4096
LEN = 256


def span_squares(inputs_block, gather_piece):
    span_count = inputs_block.shape[1] // LEN
    left_block = inputs_block.reshape(inputs_block.shape[0], span_count, LEN)
    right_block = gather_piece.reshape(gather_piece.shape[0], span_count, LEN)
    products = jnp.einsum(
        "icl,ocl->cio", left_block, right_block, preferred_element_type=jnp.float32
    )
    return jnp.sum(products * products, axis=0)


def per_device(rot_grads, rot_inputs, lengths, token_mask):
    spans_here = lengths.shape[0]
    slot_ids = jnp.arange(LEN, dtype=jnp.int32)
    inside = (slot_ids[None, :] < lengths[:, None]).astype(jnp.int32).reshape(-1)
    usable = token_mask * inside
    weighted = rot_inputs * usable.astype(jnp.bfloat16)[None, :]
    running = jnp.zeros((rot_inputs.shape[0], O), jnp.float32)
    for span_id in range(spans_here):
        inputs_part = weighted[:, span_id * LEN : (span_id + 1) * LEN]
        grads_part = rot_grads[:, span_id * LEN : (span_id + 1) * LEN]
        running = running + span_squares(
            inputs_part, lax.all_gather(grads_part, "grid", axis=0, tiled=True)
        )
    halves = lax.psum_scatter(running, "dp", scatter_dimension=1, tiled=True)
    return halves / (spans_here * lax.axis_size("dp"))


def solution(mesh):
    return jax.shard_map(
        per_device,
        mesh=mesh,
        in_specs=(
            P("grid", ("groups", "dp")),
            P("grid", ("groups", "dp")),
            P(("groups", "dp")),
            P(("groups", "dp")),
        ),
        out_specs=P(("groups", "grid"), "dp"),
        check_vma=False,
    )
```

profile of v0, /device:TPU:1, one launch (start us, length us, event | category | flops | bytes accessed | tf_op | source)
XLA Modules:
  0.0 386.7 jit_solution(7665151907215006139)
XLA Ops:
  6.5 0.0 all-gather.9.cloned.1.call-start
  6.5 2.2 fusion.7
  8.7 0.0 all-gather.9.cloned.1.call-update
  8.7 0.0 all-gather.7.cloned.1.call-start
  8.8 0.7 all-gather.7.cloned.1.call-update
  9.5 0.0 all-gather.5.cloned.1.call-start
  9.5 0.7 all-gather.5.cloned.1.call-update
  10.2 0.0 all-gather.11.cloned.1.call-start
  10.3 0.5 all-gather.11.cloned.1.call-update
  10.8 0.0 reduce-scatter.2.cloned.1.call-start
  10.8 0.7 iota_compare_fusion
  11.6 0.7 select_convert_fusion
  12.3 6.6 %broadcast_multiply_fusion.1 = bf16[3584,1024]{1,0:T(8,128)(2,1)} fusion(bf16[3584,1024]{1,0:T(8,128)(2,1)} %param.5, bf16[1024]{0:T(1024)(128)(2,1)S(1)} %select_convert_fusion), kind=kLoop, calls=%fused_computation.2 | loop fusion | flops 3670016 | bytes 14682112 | tf_op jit(solution)/shard_map/mul | solution.py:25
  18.9 40.9 %all-gather.9.cloned.1.call-done = bf16[4096,256]{1,0:T(8,128)(2,1)} async-done(((bf16[512,256]{1,0:T(8,128)(2,1)}), bf16[4096,256]{1,0:T(8,128)(2,1)}) %all-gather.9.cloned.1.call-update) | async-done | bytes 2097168 | tf_op jit(solution)/shard_map/all_gather | solution.py:31
  59.8 23.4 %fusion.1 = f32[3584,4096]{1,0:T(8,128)} fusion(bf16[4096,256]{1,0:T(8,128)(2,1)} %all-gather.9.cloned.1.call-done, bf16[3584,1024]{1,0:T(8,128)(2,1)} %broadcast_multiply_fusion.1), kind=kOutput, calls=%fused_computation.4 | convolution fusion | flops 7516192768 | bytes 62652416 | tf_op jit(solution)/shard_map/icl,ocl->cio/dot_general | solution.py:14
  83.2 26.5 %all-gather.7.cloned.1.call-done = bf16[4096,256]{1,0:T(8,128)(2,1)} async-done(((bf16[512,256]{1,0:T(8,128)(2,1)}), bf16[4096,256]{1,0:T(8,128)(2,1)}) %all-gather.7.cloned.1.call-update) | async-done | bytes 2097168 | tf_op jit(solution)/shard_map/all_gather | solution.py:31
  109.7 23.4 %fusion.3 = f32[3584,4096]{1,0:T(8,128)} fusion(bf16[4096,256]{1,0:T(8,128)(2,1)} %all-gather.7.cloned.1.call-done, bf16[3584,1024]{1,0:T(8,128)(2,1)} %broadcast_multiply_fusion.1), kind=kOutput, calls=%fused_computation.6 | convolution fusion | flops 7516192768 | bytes 62652416 | tf_op jit(solution)/shard_map/icl,ocl->cio/dot_general | solution.py:14
  133.1 26.5 %all-gather.5.cloned.1.call-done = bf16[4096,256]{1,0:T(8,128)(2,1)} async-done(((bf16[512,256]{1,0:T(8,128)(2,1)}), bf16[4096,256]{1,0:T(8,128)(2,1)}) %all-gather.5.cloned.1.call-update) | async-done | bytes 2097168 | tf_op jit(solution)/shard_map/all_gather | solution.py:31
  159.7 23.4 %fusion.5 = f32[3584,4096]{1,0:T(8,128)} fusion(bf16[4096,256]{1,0:T(8,128)(2,1)} %all-gather.5.cloned.1.call-done, bf16[3584,1024]{1,0:T(8,128)(2,1)} %broadcast_multiply_fusion.1), kind=kOutput, calls=%fused_computation.8 | convolution fusion | flops 7516192768 | bytes 62652416 | tf_op jit(solution)/shard_map/icl,ocl->cio/dot_general | solution.py:14
  183.1 26.4 %all-gather.11.cloned.1.call-done = bf16[4096,256]{1,0:T(8,128)(2,1)} async-done(((bf16[512,256]{1,0:T(8,128)(2,1)}), bf16[4096,256]{1,0:T(8,128)(2,1)}) %all-gather.11.cloned.1.call-update) | async-done | bytes 2097168 | tf_op jit(solution)/shard_map/all_gather | solution.py:31
  209.4 75.7 %multiply_add_fusion = f32[3584,4096]{1,0:T(8,128)} fusion(f32[3584,4096]{1,0:T(8,128)} %fusion.1, f32[3584,4096]{1,0:T(8,128)} %fusion.3, f32[3584,4096]{1,0:T(8,128)} %fusion.5, bf16[4096,256]{1,0:T(8,128)(2,1)} %all-gather.11.cloned.1.call-done, bf16[3584,1024]{1,0:T(8,128)(2,1)} %broadcast_multiply_fusion.1), kind=kOutput, calls=%fused_computation | convolution fusion | flops 7618953216 | bytes 238813184 | tf_op jit(solution)/shard_map/icl,ocl->cio/dot_general | solution.py:14
  285.1 0.0 reduce-scatter.2.cloned.1.call-update
  285.2 73.0 %reduce-scatter.2.cloned.1.call-done = f32[3584,2048]{1,0:T(8,128)} async-done(((f32[3584,4096]{1,0:T(8,128)}), f32[3584,2048]{1,0:T(8,128)}) %reduce-scatter.2.cloned.1.call-update) | async-done | bytes 29360144 | tf_op jit(solution)/shard_map/reduce_scatter | solution.py:33
  358.1 22.1 %broadcast_multiply_fusion = f32[3584,2048]{1,0:T(8,128)} fusion(f32[3584,2048]{1,0:T(8,128)} %reduce-scatter.2.cloned.1.call-done), kind=kLoop, calls=%fused_computation.1 | loop fusion | flops 7340032 | bytes 58720256 | tf_op jit(solution)/shard_map/div | solution.py:34
  (1 shorter events, 0.0 us)
Async XLA Ops:
  6.5 53.2 %all-gather.9.cloned.1.call-start = ((), (), s32[]{:S(2)}) async-start(), calls=%async_computation.3 | async-start | bytes 2359296 | tf_op jit(solution)/shard_map/all_gather | solution.py:31
  8.7 101.0 %all-gather.7.cloned.1.call-start = ((), (), s32[]{:S(2)}) async-start(), calls=%async_computation.2 | async-start | bytes 2359296 | tf_op jit(solution)/shard_map/all_gather | solution.py:31
  9.5 150.2 %all-gather.5.cloned.1.call-start = ((), (), s32[]{:S(2)}) async-start(), calls=%async_computation.1 | async-start | bytes 2359296 | tf_op jit(solution)/shard_map/all_gather | solution.py:31
  10.2 199.2 %all-gather.11.cloned.1.call-start = ((), (), s32[]{:S(2)}) async-start(), calls=%async_computation.4 | async-start | bytes 2359296 | tf_op jit(solution)/shard_map/all_gather | solution.py:31
  10.8 347.3 %reduce-scatter.2.cloned.1.call-start = ((), (), s32[]{:S(2)}) async-start(), calls=%async_computation.5 | async-start | bytes 88080384 | tf_op jit(solution)/shard_map/reduce_scatter | solution.py:33
Sparse Core Ops, SparseCore 0:
  9.5 50.2 all-gather.8
  61.9 47.7 all-gather.6
  111.8 47.7 all-gather.4
  161.6 47.7 all-gather.10
  285.3 72.7 reduce-scatter.1
where the time goes:
time: 387 us
  waiting for transfers between devices  195 us (50%)
  matrix products  146 us (38%)
  other arithmetic  30.1 us (8%)
  between operations  13.1 us (3%)
    dot_general x4, matrix products, span_squares(): jnp.einsum('icl,ocl->cio', left_block, right_block, preferred_element_typ...  146 us
    all_gather x4, waiting for transfers between devices, per_device(): lax.all_gather(grads_part, 'grid', axis=0, tiled=True)  120 us
    reduce_scatter x1, waiting for transfers between devices, per_device(): halves = lax.psum_scatter(running, 'dp', scatter_dimension=1, tiled=True)  73 us
    div x1, other arithmetic, per_device(): return halves / (spans_here * lax.axis_size('dp'))  22.1 us
  transfers between devices with their start and end apart: 5, of which 5 were waited for; matrix products, arithmetic and copies ran while one was open for 20% of the time, Pallas kernels for 0%

commit v1 on v0

v1 whole, which is shorter than its diff:
```python
import functools

import jax
import jax.numpy as jnp
from jax import lax
from jax.experimental import pallas as pl
from jax.experimental.pallas import tpu as pltpu
from jax.sharding import PartitionSpec as P

LEN = 256
CHUNKS = 2
MESH = pl.DeviceIdType.MESH


def grid_sides(grid_size):
    inner = 1
    while (inner * 2) * (inner * 2) <= grid_size:
        inner *= 2
    return grid_size // inner, inner


def gather_kernel(nz, ny, chunks, g_ref, x_ref, gbuf, xbuf, own_send, fwd_send, recv, local_sem, x_sems):
    grid = lax.axis_index("grid")
    core = lax.axis_index("dp")
    z = grid // ny
    y = grid % ny
    zh = nz // 2
    half = zh * ny
    rows = g_ref.shape[0] // chunks

    up, down = z < nz - 1, z > 0
    right, left = y < ny - 1, y > 0
    barrier = pltpu.get_barrier_semaphore()
    for there, target in ((up, grid + ny), (down, grid - ny), (right, grid + 1), (left, grid - 1)):
        @pl.when(there)
        def _():
            for other in range(2):
                pl.semaphore_signal(
                    barrier, inc=1, device_id={"grid": target, "dp": other}, device_id_type=MESH
                )
    pl.semaphore_signal(barrier, inc=1, device_id={"dp": 1 - core}, device_id_type=MESH)
    neighbours = sum(there.astype(jnp.int32) for there in (up, down, right, left))
    pl.semaphore_wait(barrier, 2 * neighbours + 1)

    def piece(slot, index, c):
        return gbuf.at[slot, index, pl.ds(pl.multiple_of(c * rows, rows), rows)]

    def send(src, slot, index, c, sem, target, target_core):
        return pltpu.make_async_remote_copy(
            src_ref=src,
            dst_ref=piece(slot, index, c),
            send_sem=sem,
            recv_sem=recv.at[slot, index, c],
            device_id={"grid": target, "dp": target_core},
            device_id_type=MESH,
        )

    owner = z // zh
    own_slot = jnp.where(core == owner, 0, 1)
    own_index = grid - owner * half

    def own_copies(c):
        src = g_ref.at[pl.ds(pl.multiple_of(c * rows, rows), rows)]
        return [
            (there, send(src, own_slot, own_index, c, own_send.at[c, k], target, owner))
            for k, (there, target) in enumerate(
                ((up, grid + ny), (down, grid - ny), (right, grid + 1), (left, grid - 1), (core != owner, grid))
            )
        ]

    local = pltpu.make_async_copy(g_ref, gbuf.at[0, own_index], local_sem)

    @pl.loop(0, chunks)
    def _(c):
        for there, copy in own_copies(c):
            @pl.when(there)
            def _():
                copy.start()

    x_copy = pltpu.make_async_remote_copy(
        src_ref=x_ref, dst_ref=xbuf, send_sem=x_sems.at[0], recv_sem=x_sems.at[1],
        device_id={"dp": 1 - core}, device_id_type=MESH,
    )
    x_copy.start()

    @pl.when(core == owner)
    def _():
        local.start()

    def column_copies(step, sign, q):
        c, slot = q // 2, q % 2
        index = (z - sign * step) * ny + y - core * half
        src = piece(slot, index, c)
        onward = z + sign
        return [
            (there, send(src, slot, index, c, fwd_send.at[slot, index, c, k], target, core))
            for k, (there, target) in enumerate(
                (((onward >= 0) & (onward < nz), grid + sign * ny), (right, grid + 1), (left, grid - 1))
            )
        ]

    def row_copies(step, sign, q):
        j, c, slot = q // (2 * chunks), (q // 2) % chunks, q % 2
        zi = jnp.where(z <= core * zh, j, zh - 1 - j)
        index = zi * ny + y - sign * step
        onward = y + sign
        return [
            ((onward >= 0) & (onward < ny), send(
                piece(slot, index, c), slot, index, c, fwd_send.at[slot, index, c, 0], grid + sign, core))
        ]

    def walk(act):
        for step in range(1, nz):
            for sign in (1, -1):
                source = z - sign * step

                @pl.when((source >= core * zh) & (source < core * zh + zh))
                def _():
                    @pl.loop(0, 2 * chunks)
                    def _(q):
                        act(column_copies(step, sign, q))
        for step in range(1, ny):
            for sign in (1, -1):
                source = y - sign * step

                @pl.when((source >= 0) & (source < ny))
                def _():
                    @pl.loop(0, zh * 2 * chunks)
                    def _(q):
                        act(row_copies(step, sign, q))

    def forward(copies):
        copies[0][1].wait_recv()
        for there, copy in copies:
            @pl.when(there)
            def _():
                copy.start()

    def finish(copies):
        for there, copy in copies:
            @pl.when(there)
            def _():
                copy.wait_send()

    walk(forward)

    @pl.when(core == owner)
    def _():
        @pl.loop(0, chunks)
        def _(c):
            send(piece(1, own_index, c), 1, own_index, c, own_send.at[c, 4], grid, 1 - core).wait_recv()
        local.wait()

    @pl.loop(0, chunks)
    def _(c):
        finish(own_copies(c))

    walk(finish)
    x_copy.wait()


def square_kernel(scale, g_ref, own_ref, peer_ref, out_ref):
    width = 256
    for at in range(0, out_ref.shape[1], width):
        total = None
        for which, x_ref in enumerate((own_ref, peer_ref)):
            for start in range(0, x_ref.shape[1], LEN):
                product = lax.dot_general(
                    x_ref[:, start:start + LEN],
                    g_ref[which, at:at + width, start:start + LEN],
                    (((1,), (1,)), ((), ())),
                    preferred_element_type=jnp.float32,
                )
                square = product * product
                total = square if total is None else total + square
        out_ref[:, at:at + width] = total * scale


def per_device(rot_grads, rot_inputs, lengths, token_mask):
    nz, ny = grid_sides(lax.axis_size("grid"))
    rows, tokens = rot_grads.shape
    features = rot_inputs.shape[0]
    half = nz * ny // 2
    chunks = CHUNKS if rows % (CHUNKS * 128) == 0 else 1
    slot_ids = jnp.arange(LEN, dtype=jnp.int32)
    inside = (slot_ids[None, :] < lengths[:, None]).astype(jnp.int32).reshape(-1)
    usable = token_mask * inside
    weighted = rot_grads * usable.astype(jnp.bfloat16)[None, :]

    dma = pltpu.SemaphoreType.DMA
    gathered, peer_inputs = pl.pallas_call(
        functools.partial(gather_kernel, nz, ny, chunks),
        out_shape=(
            jax.ShapeDtypeStruct((2, half, rows, tokens), jnp.bfloat16),
            jax.ShapeDtypeStruct((features, tokens), jnp.bfloat16),
        ),
        in_specs=[pl.BlockSpec(memory_space=pl.ANY)] * 2,
        out_specs=[pl.BlockSpec(memory_space=pl.ANY)] * 2,
        scratch_shapes=[
            dma((chunks, 5)),
            dma((2, half, chunks, 3)),
            dma((2, half, chunks)),
            dma,
            dma((2,)),
        ],
        compiler_params=pltpu.CompilerParams(collective_id=0, has_side_effects=True),
        name="gather",
    )(weighted, rot_inputs)

    columns = half * rows
    gathered = gathered.reshape(2, columns, tokens)
    tile = next(t for t in (512, 448, 256, 64, 8) if features % t == 0)
    spans = lengths.shape[0] * lax.axis_size("dp")
    return pl.pallas_call(
        functools.partial(square_kernel, 1.0 / spans),
        grid=(features // tile,),
        out_shape=jax.ShapeDtypeStruct((features, columns), jnp.float32),
        in_specs=[
            pl.BlockSpec((2, columns, tokens), lambda i: (0, 0, 0), pipeline_mode=pl.Buffered(1)),
            pl.BlockSpec((tile, tokens), lambda i: (i, 0)),
            pl.BlockSpec((tile, tokens), lambda i: (i, 0)),
        ],
        out_specs=pl.BlockSpec((tile, columns), lambda i: (i, 0)),
        compiler_params=pltpu.CompilerParams(vmem_limit_bytes=48 * 2**20),
        name="squares",
    )(gathered, rot_inputs, peer_inputs)


def solution(mesh):
    return jax.shard_map(
        per_device,
        mesh=mesh,
        in_specs=(
            P("grid", ("groups", "dp")),
            P("grid", ("groups", "dp")),
            P(("groups", "dp")),
            P(("groups", "dp")),
        ),
        out_specs=P(("groups", "grid"), "dp"),
        check_vma=False,
    )
```

time: 387 us -> 138 us (0.36)
  waiting for transfers between devices: 195 us -> 0 us
  matrix products: 146 us -> 0 us
  Pallas kernels: 0 us -> 134 us
  other arithmetic: 30.1 us -> 3.68 us
  between operations: 13.1 us -> 0.01 us
    dot_general x4 -> x0, matrix products: 146 us -> none  [span_squares(): jnp.einsum('icl,ocl->cio', left_block, right_block, preferred_element_typ...]
    pallas_call x0 -> x2, Pallas kernels: none -> 134 us  [the longest x1 96.1 us: per_device(): pl.pallas_call(functools.partial(gather_kernel, nz, ny, chunks), out_shap...]
    all_gather x4 -> x0, waiting for transfers between devices: 120 us -> none  [per_device(): lax.all_gather(grads_part, 'grid', axis=0, tiled=True)]
    reduce_scatter x1 -> x0, waiting for transfers between devices: 73 us -> none  [per_device(): halves = lax.psum_scatter(running, 'dp', scatter_dimension=1, tiled=True)]
    div x1 -> x0, other arithmetic: 22.1 us -> none  [per_device(): return halves / (spans_here * lax.axis_size('dp'))]
    mul x1, other arithmetic: 6.6 us -> 2.26 us  [per_device(): weighted = rot_grads * usable.astype(jnp.bfloat16)[None, :]]
  transfers between devices with their start and end apart: 5 -> 0, of which waited for: 5 -> 0; matrix products, arithmetic and copies ran while one was open for 20% -> 0% of each run, Pallas kernels for 0% -> 0%
where the time goes in v1:
time: 138 us
  Pallas kernels  134 us (97%)
  other arithmetic  3.68 us (3%)
    pallas_call x1, Pallas kernels, per_device(): pl.pallas_call(functools.partial(gather_kernel, nz, ny, chunks), out_shap...  96.1 us
    pallas_call x1, Pallas kernels, per_device(): pl.pallas_call(functools.partial(square_kernel, 1.0 / spans), grid=(featu...  38.3 us

profile of v1, /device:TPU:1, one launch (start us, length us, event | category | flops | bytes accessed | tf_op | source)
XLA Modules:
  0.0 138.1 jit_solution(14769591719608093717)
XLA Ops:
  0.0 0.7 iota_compare_fusion
  0.7 0.7 select_convert_fusion
  1.4 2.3 %broadcast_multiply_fusion.g_ref = bf16[512,1024]{1,0:T(8,128)(2,1)} fusion(bf16[512,1024]{1,0:T(8,128)(2,1)} %param.4, bf16[1024]{0:T(1024)(128)(2,1)S(1)} %select_convert_fusion), kind=kLoop, calls=%fused_computation | loop fusion | flops 524288 | bytes 2099200 | tf_op jit(solution)/shard_map/mul | solution.py:188
  3.7 96.1 %gather.1 = (bf16[2,4,512,1024]{3,2,1,0:T(8,128)(2,1)}, bf16[3584,1024]{1,0:T(8,128)(2,1)}) custom-call(bf16[512,1024]{1,0:T(8,128)(2,1)} %broadcast_multiply_fusion.g_ref, bf16[3584,1024]{1,0:T(8,128)(2,1)} %own_ref.1), custom_call_target="tpu_custom_call" | custom-call | tf_op jit(solution)/shard_map/gather/pallas_call | solution.py:191
  99.8 38.3 %squares.1 = f32[3584,2048]{1,0:T(8,128)} custom-call(bf16[2,2048,1024]{2,1,0:T(8,128)(2,1)} %bitcast.1, bf16[3584,1024]{1,0:T(8,128)(2,1)} %own_ref.1, bf16[3584,1024]{1,0:T(8,128)(2,1)} %get-tuple-element.8.peer_ref), custom_call_target="tpu_custom_call" | custom-call | tf_op jit(solution)/shard_map/squares/pallas_call | solution.py:214
  (1 shorter events, 0.0 us)

commit v2 on v1

--- a/solution.py
+++ b/solution.py
@@ -9,6 +9,8 @@
 
 LEN = 256
 CHUNKS = 2
+TAIL_TILE = 256
+GRANT = 18 * 2**20
 MESH = pl.DeviceIdType.MESH
 
 
@@ -176,10 +178,341 @@
         out_ref[:, at:at + width] = total * scale
 
 
+def pieces_of(rows):
+    if rows % 512:
+        return ((0, rows, False),)
+    unit = rows // 512
+    cuts = (0, 32, 128, 256, 384, 512)
+    return tuple((a * unit, (b - a) * unit, a == 0) for a, b in zip(cuts, cuts[1:]))
+
+
+def squares(scale, tokens, x_of, g_of):
+    total = None
+    for which in range(2):
+        for start in range(0, tokens, LEN):
+            product = lax.dot_general(
+                x_of(which, start),
+                g_of(which, start),
+                (((1,), (1,)), ((), ())),
+                preferred_element_type=jnp.float32,
+            )
+            square = product * product
+            total = square if total is None else total + square
+    return total * scale
+
+
+def gather_squares_kernel(
+    nz, tile, scale, g_ref, mask_ref, lengths_ref, x_ref, gbuf, xbuf, done_ref,
+    masked, held, x_tiles, outs, own_send, fwd_send, recv, local_sem, x_sems, held_sems, tile_sems, peer_sems, out_sems,
+):
+    ny = 2
+    grid = lax.axis_index("grid")
+    core = lax.axis_index("dp")
+    z = grid // ny
+    y = grid % ny
+    zh = nz // 2
+    half = zh * ny
+    rows, tokens = g_ref.shape
+    pieces = pieces_of(rows)
+    across = grid + 1 - 2 * y
+
+    up, down = z < nz - 1, z > 0
+    barrier = pltpu.get_barrier_semaphore()
+    for other in range(2):
+        @pl.when(up)
+        def _():
+            pl.semaphore_signal(barrier, inc=1, device_id={"grid": grid + ny, "dp": other}, device_id_type=MESH)
+
+        @pl.when(down)
+        def _():
+            pl.semaphore_signal(barrier, inc=1, device_id={"grid": grid - ny, "dp": other}, device_id_type=MESH)
+
+        pl.semaphore_signal(barrier, inc=1, device_id={"grid": across, "dp": other}, device_id_type=MESH)
+    pl.semaphore_signal(barrier, inc=1, device_id={"dp": 1 - core}, device_id_type=MESH)
+
+    for start in range(0, tokens, LEN):
+        slot_ids = lax.broadcasted_iota(jnp.int32, (1, LEN), 1)
+        usable = jnp.where(slot_ids < lengths_ref[start // LEN], mask_ref[:, start:start + LEN], 0)
+        weights = usable.astype(jnp.float32).astype(jnp.bfloat16)
+        masked[:, start:start + LEN] = g_ref[:, start:start + LEN] * weights
+
+    pl.semaphore_wait(barrier, 2 * (up.astype(jnp.int32) + down.astype(jnp.int32)) + 3)
+
+    def part(slot, index, c):
+        return gbuf.at[slot, index, pl.ds(pieces[c][0], pieces[c][1])]
+
+    def send(src, slot, index, c, sem, target, target_core):
+        return pltpu.make_async_remote_copy(
+            src_ref=src,
+            dst_ref=part(slot, index, c),
+            send_sem=sem,
+            recv_sem=recv.at[slot, index, c],
+            device_id={"grid": target, "dp": target_core},
+            device_id_type=MESH,
+        )
+
+    owner = z // zh
+    own_slot = jnp.where(core == owner, 0, 1)
+    own_index = grid - owner * half
+
+    def own_copies(c):
+        src = masked.at[pl.ds(pieces[c][0], pieces[c][1])]
+        return [
+            (there, send(src, own_slot, own_index, c, own_send.at[c, k], target, owner))
+            for k, (there, target) in enumerate(
+                ((None, across), (up, grid + ny), (down, grid - ny), (core != owner, grid))
+            )
+        ]
+
+    def each(copies, act):
+        for there, copy in copies:
+            if there is None:
+                act(copy)
+            else:
+                pl.when(there)(functools.partial(act, copy))
+
+    for c in range(len(pieces)):
+        each(own_copies(c), lambda copy: copy.start())
+
+    x_copy = pltpu.make_async_remote_copy(
+        src_ref=x_ref, dst_ref=xbuf, send_sem=x_sems.at[0], recv_sem=x_sems.at[1],
+        device_id={"dp": 1 - core}, device_id_type=MESH,
+    )
+    x_copy.start()
+    local = pltpu.make_async_copy(masked, held.at[0], local_sem)
+
+    @pl.when(core == owner)
+    def _():
+        local.start()
+
+    def onward(slot, index, c, source, own_column):
+        src = part(slot, index, c)
+        y_first = pieces[c][2]
+        if own_column or y_first:
+            yield up & (z >= source), send(src, slot, index, c, fwd_send.at[slot, index, c, 0], grid + ny, core)
+            yield down & (z <= source), send(src, slot, index, c, fwd_send.at[slot, index, c, 1], grid - ny, core)
+        if own_column and not y_first:
+            yield None, send(src, slot, index, c, fwd_send.at[slot, index, c, 2], across, core)
+
+    def arrived(slot, index, c):
+        send(part(slot, index, c), slot, index, c, fwd_send.at[slot, index, c, 2], across, core).wait_recv()
+
+    near = jnp.where(z <= core * zh, 0, 1)
+    far = 1 - near
+
+    def group(zi, c, own_column, wait_first, act):
+        source = core * zh + zi
+        index = zi * ny + (y if own_column else 1 - y)
+
+        def step():
+            @pl.loop(0, 2)
+            def _(slot):
+                if wait_first:
+                    arrived(slot, index, c)
+                each(onward(slot, index, c, source, own_column), act)
+
+        if own_column:
+            pl.when(source != z)(step)
+        else:
+            step()
+
+    groups = []
+    for c in range(len(pieces)):
+        groups.append((c, True))
+        if pieces[c][2]:
+            groups.append((c, False))
+
+    def take(zi, which):
+        group(zi, *groups[which], True, lambda copy: copy.start())
+
+    def take_rest(zi):
+        for c in range(len(pieces)):
+            if not pieces[c][2]:
+                @pl.loop(0, 2)
+                def _(slot):
+                    arrived(slot, zi * ny + 1 - y, c)
+
+    def hold(zi, column, mine):
+        for slot in range(2):
+            copy = pltpu.make_async_copy(gbuf.at[slot, zi * ny + column], held.at[slot], held_sems.at[slot])
+            if slot == 0 and mine is not None:
+                pl.when(jnp.logical_not(mine))(lambda copy=copy: copy.start())
+            else:
+                copy.start()
+        for slot in range(2):
+            copy = pltpu.make_async_copy(gbuf.at[slot, zi * ny + column], held.at[slot], held_sems.at[slot])
+            if slot == 0 and mine is not None:
+                pl.when(jnp.logical_not(mine))(lambda copy=copy: copy.wait())
+            else:
+                copy.wait()
+
+    tiles = x_ref.shape[0] // tile
+    width = min(256, rows)
+
+    def rows_of(i):
+        return pl.ds(pl.multiple_of(i * tile, tile), tile)
+
+    def tiles_in(i):
+        return (
+            pltpu.make_async_copy(x_ref.at[rows_of(i)], x_tiles.at[0, i % 2], tile_sems.at[i % 2]),
+            pltpu.make_async_copy(xbuf.at[rows_of(i)], x_tiles.at[1, i % 2], peer_sems.at[i % 2]),
+        )
+
+    def compute(column, hooks):
+        def tile_out(i):
+            columns = pl.ds(pl.multiple_of(column * rows, 128), rows)
+            return pltpu.make_async_copy(outs.at[i % 2], done_ref.at[rows_of(i), columns], out_sems.at[i % 2])
+
+        for copy in tiles_in(0):
+            copy.start()
+
+        @pl.loop(0, tiles)
+        def _(i):
+            @pl.when(i + 1 < tiles)
+            def _():
+                for copy in tiles_in(i + 1):
+                    copy.start()
+
+            for when, which in hooks:
+                @pl.when(i == when)
+                def _():
+                    take(far, which)
+
+            @pl.when(i >= 2)
+            def _():
+                tile_out(i - 2).wait()
+
+            for copy in tiles_in(i):
+                copy.wait()
+            for at in range(0, rows, width):
+                outs[i % 2, :, at:at + width] = squares(
+                    scale, tokens,
+                    lambda which, start: x_tiles[which, i % 2, :, start:start + LEN],
+                    lambda which, start: held[which, at:at + width, start:start + LEN],
+                )
+            tile_out(i).start()
+
+        for i in range(max(0, tiles - 2), tiles):
+            tile_out(i).wait()
+
+    for which in range(len(groups)):
+        take(near, which)
+    mine = core == owner
+
+    @pl.when(mine)
+    def _():
+        for c in range(len(pieces)):
+            arrived(1, own_index, c)
+        local.wait()
+
+    hold(near, y, mine)
+    x_copy.wait_recv()
+    early = min(2, len(groups))
+    last = tiles - 1
+    compute(y, [(min(3 * (k + 1), last), k) for k in range(early)])
+    take_rest(near)
+    hold(near, 1 - y, None)
+    compute(1 - y, [(min(1 + 2 * k, last), early + k) for k in range(len(groups) - early)])
+    take_rest(far)
+
+    for c in range(len(pieces)):
+        each(own_copies(c), lambda copy: copy.wait_send())
+    for zi in range(zh):
+        for c, own_column in groups:
+            group(zi, c, own_column, False, lambda copy: copy.wait_send())
+    x_copy.wait_send()
+
+
+def finish_kernel(scale, near_ref, g_ref, own_ref, peer_ref, done_ref, out_ref):
+    ny, rows, tokens = g_ref.shape[2:]
+    near = near_ref[0]
+    width = min(256, rows)
+    out_ref[:, pl.ds(pl.multiple_of(near * ny * rows, 128), ny * rows)] = done_ref[...]
+    for column in range(ny):
+        for at in range(0, rows, width):
+            start_at = pl.multiple_of(((1 - near) * ny + column) * rows + at, 128)
+            out_ref[:, pl.ds(start_at, width)] = squares(
+                scale, tokens,
+                lambda which, start: (peer_ref if which else own_ref)[:, start:start + LEN],
+                lambda which, start: g_ref[which, 0, column, at:at + width, start:start + LEN],
+            )
+
+
+def overlapped(nz, rot_grads, rot_inputs, lengths, token_mask):
+    ny = 2
+    zh = nz // 2
+    rows, tokens = rot_grads.shape
+    features = rot_inputs.shape[0]
+    tile = next(t for t in (512, 448, 256, 64, 8) if features % t == 0)
+    scale = 1.0 / (lengths.shape[0] * lax.axis_size("dp"))
+    count = len(pieces_of(rows))
+    dma = pltpu.SemaphoreType.DMA
+    anywhere = pl.BlockSpec(memory_space=pl.ANY)
+    gathered, peer_inputs, done = pl.pallas_call(
+        functools.partial(gather_squares_kernel, nz, tile, scale),
+        out_shape=(
+            jax.ShapeDtypeStruct((2, zh * ny, rows, tokens), jnp.bfloat16),
+            jax.ShapeDtypeStruct((features, tokens), jnp.bfloat16),
+            jax.ShapeDtypeStruct((features, ny * rows), jnp.float32),
+        ),
+        in_specs=[
+            pl.BlockSpec(memory_space=pltpu.VMEM),
+            pl.BlockSpec(memory_space=pltpu.VMEM),
+            pl.BlockSpec(memory_space=pltpu.SMEM),
+            anywhere,
+        ],
+        out_specs=[anywhere] * 3,
+        scratch_shapes=[
+            pltpu.VMEM((rows, tokens), jnp.bfloat16),
+            pltpu.VMEM((2, rows, tokens), jnp.bfloat16),
+            pltpu.VMEM((2, 2, tile, tokens), jnp.bfloat16),
+            pltpu.VMEM((2, tile, rows), jnp.float32),
+            dma((count, 4)),
+            dma((2, zh * ny, count, 3)),
+            dma((2, zh * ny, count)),
+            dma,
+            dma((2,)),
+            dma((2,)),
+            dma((2,)),
+            dma((2,)),
+            dma((2,)),
+        ],
+        compiler_params=pltpu.CompilerParams(
+            collective_id=0, has_side_effects=True, vmem_limit_bytes=GRANT
+        ),
+        name="gather_squares",
+    )(rot_grads, token_mask.reshape(1, tokens), lengths, rot_inputs)
+
+    grid = lax.axis_index("grid")
+    near = (grid // ny > lax.axis_index("dp") * zh).astype(jnp.int32).reshape(1)
+    tile = next(t for t in (TAIL_TILE, 448, 256, 64, 8) if features % t == 0)
+    return pl.pallas_call(
+        functools.partial(finish_kernel, scale),
+        out_shape=jax.ShapeDtypeStruct((features, zh * ny * rows), jnp.float32),
+        grid_spec=pltpu.PrefetchScalarGridSpec(
+            num_scalar_prefetch=1,
+            grid=(features // tile,),
+            in_specs=[
+                pl.BlockSpec(
+                    (2, 1, ny, rows, tokens), lambda i, at: (0, 1 - at[0], 0, 0, 0), pipeline_mode=pl.Buffered(1)
+                ),
+                pl.BlockSpec((tile, tokens), lambda i, at: (i, 0)),
+                pl.BlockSpec((tile, tokens), lambda i, at: (i, 0)),
+                pl.BlockSpec((tile, ny * rows), lambda i, at: (i, 0)),
+            ],
+            out_specs=pl.BlockSpec((tile, zh * ny * rows), lambda i, at: (i, 0)),
+        ),
+        compiler_params=pltpu.CompilerParams(vmem_limit_bytes=GRANT),
+        name="finish",
+    )(near, gathered.reshape(2, zh, ny, rows, tokens), rot_inputs, peer_inputs, done)
+
+
 def per_device(rot_grads, rot_inputs, lengths, token_mask):
     nz, ny = grid_sides(lax.axis_size("grid"))
     rows, tokens = rot_grads.shape
     features = rot_inputs.shape[0]
+    if ny == 2 and nz == 4 and rows % 128 == 0:
+        return overlapped(nz, rot_grads, rot_inputs, lengths, token_mask)
     half = nz * ny // 2
     chunks = CHUNKS if rows % (CHUNKS * 128) == 0 else 1
     slot_ids = jnp.arange(LEN, dtype=jnp.int32)

time: 138 us -> 138 us (level); the launches traced: 138 us -> 136 us
  local copies, waits for them, and re-layouts: 0.01 us -> 5.65 us
  Pallas kernels: 134 us -> 130 us
  other arithmetic: 3.68 us -> 0 us
    unnamed x0 -> x10, local copies, waits for them, and re-layouts: none -> 5.65 us
    pallas_call x2, Pallas kernels: 134 us -> 130 us  [the longest x1 104 us: overlapped(): pl.pallas_call(functools.partial(gather_squares_kernel, nz, tile, scale),...]
    mul x1 -> x0, other arithmetic: 2.26 us -> none  [per_device(): weighted = rot_grads * usable.astype(jnp.bfloat16)[None, :]]
where the time goes in v2:
time: 138 us; the launch traced here: 136 us
  Pallas kernels  130 us (94%)
  local copies, waits for them, and re-layouts  5.65 us (4%)
    pallas_call x1, Pallas kernels, overlapped(): pl.pallas_call(functools.partial(gather_squares_kernel, nz, tile, scale),...  104 us
    pallas_call x1, Pallas kernels, overlapped(): pl.pallas_call(functools.partial(finish_kernel, scale), out_shape=jax.Sha...  26.7 us
    unnamed x10, local copies, waits for them, and re-layouts  5.65 us

profile of v2, /device:TPU:1, one launch (start us, length us, event | category | flops | bytes accessed | tf_op | source)
XLA Modules:
  0.0 136.0 jit_solution(2200187286754051093)
XLA Ops:
  0.0 0.0 copy-start
  0.0 3.1 %copy-done = bf16[3584,1024]{1,0:T(8,128)(2,1)S(1)} copy-done((bf16[3584,1024]{1,0:T(8,128)(2,1)S(1)}, bf16[3584,1024]{1,0:T(8,128)(2,1)}, u32[]{:S(2)}) %copy-start) | copy-done | bytes 7340056
  3.1 0.0 copy-start.2
  3.1 1.2 copy-done.2
  4.3 0.0 copy-start.3
  4.3 0.7 copy-done.3
  5.0 0.0 copy-start.4
  5.0 0.7 copy-done.4
  5.7 0.0 copy-start.1
  5.7 103.6 %gather_squares.1 = (bf16[2,4,512,1024]{3,2,1,0:T(8,128)(2,1)S(1)}, bf16[3584,1024]{1,0:T(8,128)(2,1)S(1)}, f32[3584,1024]{1,0:T(8,128)}) custom-call(bf16[512,1024]{1,0:T(8,128)(2,1)S(1)} %copy-done.2, s32[1,1024]{1,0:T(1,128)S(1)} %bitcast.4, s32[4]{0:T(128)S(1)} %copy-done.4, bf16[3584,1024]{1,0:T(8,128)(2,1)S(1)} %copy-done), custom_call_target="tpu_custom_call" | custom-call | tf_op jit(solution)/shard_map/gather_squares/pallas_call | solution.py:451
  109.3 0.0 copy-done.1
  109.3 26.7 %finish.1 = f32[3584,2048]{1,0:T(8,128)} custom-call(s32[1]{0:T(128)} %bitcast.near_ref, bf16[2,2,2,512,1024]{4,3,2,1,0:T(8,128)(2,1)S(1)} %bitcast.3, bf16[3584,1024]{1,0:T(8,128)(2,1)S(1)} %copy-done.1, bf16[3584,1024]{1,0:T(8,128)(2,1)S(1)} %get-tuple-element.9.peer_ref, f32[3584,1024]{1,0:T(8,128)} %get-tuple-element.10.done_ref), custom_call_target="tpu_custom_call" | custom-call | tf_op jit(solution)/shard_map/finish/pallas_call | solution.py:489
Async XLA Ops:
  0.0 3.1 %copy-start = (bf16[3584,1024]{1,0:T(8,128)(2,1)S(1)}, bf16[3584,1024]{1,0:T(8,128)(2,1)}, u32[]{:S(2)}) copy-start(bf16[3584,1024]{1,0:T(8,128)(2,1)} %own_ref.1) | copy-start | bytes 22020100
  3.1 1.2 copy-start.2
  4.3 0.7 copy-start.3
  5.0 0.7 copy-start.4
  5.7 103.6 %copy-start.1 = (bf16[3584,1024]{1,0:T(8,128)(2,1)S(1)}, bf16[3584,1024]{1,0:T(8,128)(2,1)}, u32[]{:S(2)}) copy-start(bf16[3584,1024]{1,0:T(8,128)(2,1)} %own_ref.1) | copy-start | bytes 22020100
